TPU v7x, 32 devices: a whole 2x2x4 slice. The times are simulated.
32 devices in a mesh: grp: 2 (over y), mode: 4 (over z), site: 4 (over x, core).
Axes of the slice: x: 2, y: 2, z: 4, core: 2. Of those that a mesh axis runs over, the one named last changes fastest.
Arguments:
- w_modes: bfloat16 [2, 1024, 12, 256], P(None, ('grp', 'mode'), None, 'site'), parts along dimension 1, may hold values from -6 to 6
- v_modes: bfloat16 [2, 512, 12, 256], P(None, ('grp', 'mode'), None, 'site'), parts along dimension 1, may hold values from -0.078125 to 0.078125
- momenta: int32 [4, 3], replicated, may hold values from -2 to 2
Outputs:
- meson: float32 [2, 4, 1024, 192], P(None, None, ('grp', 'mode', 'site')), parts along dimension 2
There are 2 independent parts, one for each index of `grp`. A program takes and returns all parts, laid end to end along the dimension named above; an argument that names none is the same for every part. Nothing has to cross between parts.
All inputs are finite; a program needn't handle non-finite values.
Results may differ from a plain program's by a relative error of at most 0.0028.
Values may be sent and summed in bfloat16 or wider, within the bound.
No kernel may reach another device: no remote copies, remote signals or barrier semaphores. Data moves between devices by JAX's collectives and lax.ppermute only.
A program may use at most 64 MiB of HBM per device.

v0:
```python
import jax
import jax.numpy as jnp
import numpy as np
from jax import lax
from jax.sharding import PartitionSpec as P

LAT = 96
REACH = 4


def shifted(value, axis, steps):
    count = lax.axis_size(axis)
    pairs = [(source, (source + steps) % count) for source in range(count)]
    return lax.ppermute(value, axis, pairs)


def make_phase(momenta, first, count):
    index = first + jnp.arange(count, dtype=jnp.int32)
    xcoord = index % LAT
    ycoord = index // LAT % LAT
    zcoord = index // (LAT * LAT)
    total = (
        momenta[:, 0:1] * xcoord[None, :]
        + momenta[:, 1:2] * ycoord[None, :]
        + momenta[:, 2:3] * zcoord[None, :]
    )
    wound = total % LAT
    angle = -2.0 * np.pi / LAT * wound.astype(jnp.float32)
    return (jnp.cos(angle), jnp.sin(angle))


def apply_gamma(vectors):
    count = vectors.shape[1]
    sites = vectors.shape[3]
    shaped = vectors.reshape(2, count, 4, 3, sites)
    signs = jnp.array([-1.0, 1.0, 1.0, -1.0], jnp.float32)
    flipped = shaped[:, :, ::-1].astype(jnp.float32) * signs[None, None, :, None, None]
    return flipped.astype(jnp.bfloat16).reshape(2, count, 12, sites)


def phased_rows(wblock, cosine, sine):
    wreal = wblock[0].astype(jnp.float32)
    wimag = wblock[1].astype(jnp.float32)
    creal = cosine[:, None, None, :]
    cimag = sine[:, None, None, :]
    areal = wreal[None] * creal + wimag[None] * cimag
    aimag = wreal[None] * cimag - wimag[None] * creal
    rows = areal.shape[0] * areal.shape[1]
    width = areal.shape[2] * areal.shape[3]
    return jnp.concatenate([areal.reshape(rows, width), aimag.reshape(rows, width)], axis=0).astype(
        jnp.bfloat16
    )


def contract(lhs, block, nph, wrows):
    width = block.shape[2] * block.shape[3]
    rhs = jnp.concatenate([block[0].reshape(-1, width), block[1].reshape(-1, width)], axis=0)
    prod = lax.dot_general(lhs, rhs, (((1,), (1,)), ((), ())), preferred_element_type=jnp.float32)
    half_rows = nph * wrows
    half_cols = block.shape[1]
    real_part = prod[:half_rows, :half_cols] - prod[half_rows:, half_cols:]
    imag_part = prod[:half_rows, half_cols:] + prod[half_rows:, :half_cols]
    return jnp.stack([real_part, imag_part]).reshape(2, nph, wrows, half_cols)


def shards(w_modes, v_modes, momenta):
    wrows = w_modes.shape[1]
    sites = w_modes.shape[3]
    vrows = v_modes.shape[1]
    nph = momenta.shape[0]
    nmode = lax.axis_size("mode")
    reach = min(REACH, (nmode - 1) // 2)
    band_width = (2 * reach + 1) * vrows
    first = lax.axis_index("site") * sites
    cosine, sine = make_phase(momenta, first, sites)
    lhs = phased_rows(w_modes, cosine, sine)
    resident = apply_gamma(v_modes)
    accum = jnp.zeros((2, nph, wrows, band_width), jnp.float32)

    def handle(accum, block, offset):
        column = (offset + reach) * vrows
        part = contract(lhs, block, nph, wrows)
        return accum.at[:, :, :, column : column + vrows].set(part)

    moving = shifted(resident, "mode", reach)
    accum = handle(accum, moving, -reach)
    for step in range(1, 2 * reach + 1):
        moving = shifted(moving, "mode", -1)
        accum = handle(accum, moving, step - reach)
    return lax.psum_scatter(accum, "site", scatter_dimension=2, tiled=True)


def solution(mesh):
    placed = (P(None, ("grp", "mode"), None, "site"), P(None, ("grp", "mode"), None, "site"), P())
    return jax.shard_map(
        shards,
        mesh=mesh,
        in_specs=placed,
        out_specs=P(None, None, ("grp", "mode", "site"), None),
        check_vma=False,
    )
```

profile of v0, /device:TPU:0, one launch (start us, length us, event | category | flops | bytes accessed | tf_op | source)
XLA Modules:
  0.0 82.9 jit_solution(3586590455102904826)
XLA Ops:
  6.5 1.2 %multiply_convert_fusion = bf16[2,64,4,3,64]{4,1,3,2,0:T(8,128)(2,1)S(1)} fusion(f32[4]{0:T(128)} %constant.127.clone, bf16[2,64,4,3,64]{4,1,3,2,0:T(8,128)(2,1)} %bitcast.37), kind=kLoop, calls=%fused_computation.6 | loop fusion | flops 294912 | bytes 393232 | tf_op jit(solution)/shard_map/convert_element_type | solution.py:38
  7.7 3.1 %collective-permute-start = (bf16[2,64,12,64]{3,1,2,0:T(8,128)(2,1)S(1)}, bf16[2,64,12,64]{3,1,2,0:T(8,128)(2,1)S(1)}, u32[]{:S(2)}, u32[]{:S(2)}) collective-permute-start(bf16[2,64,12,64]{3,1,2,0:T(8,128)(2,1)S(1)} %bitcast.38), channel_id=1, source_target_pairs={{0,4},{4,8},{8,12},{12,0},{1,5},{5,9},{9,13},{13,1},{2,6},{6,10},{... | collective-permute-start | bytes 589832 | tf_op jit(solution)/shard_map/ppermute | solution.py:14
  10.9 1.0 %slice_reduce_fusion.2 = (s32[4]{0:T(128)S(1)}, s32[4]{0:T(128)S(1)}, s32[4]{0:T(128)S(1)}) fusion(s32[4,3]{1,0:T(4,128)} %param.12), kind=kLoop, calls=%fused_computation.35 | loop fusion | bytes 96 | tf_op jit(solution)/shard_map/slice | solution.py:23
  12.2 1.1 %bitcast_convert_fusion.1 = (f32[128,12,64]{0,2,1:T(8,128)S(1)}, f32[128,12,64]{0,2,1:T(8,128)S(1)}) fusion(bf16[2,128,12,64]{1,3,2,0:T(8,128)(2,1)} %param.10), kind=kLoop, calls=%fused_computation.22 | loop fusion | flops 196608 | bytes 1179648 | tf_op jit(solution)/shard_map/mul | solution.py:46
  13.3 0.9 %subtract_convert_fusion = (bf16[4,128,12,64]{1,0,3,2:T(4,128)(2,1)S(1)}, bf16[4,128,12,64]{1,0,3,2:T(4,128)(2,1)S(1)}) fusion(f32[4,64]{0,1:T(8,128)S(1)} %copy.33, f32[128,12,64]{0,2,1:T(8,128)S(1)} %get-tuple-element.59, f32[4,64]{0,1:T(8,128)S(1)} %copy.32, f32[128,12,64]{0,2,1:T(8,128)S(1)} %get-tuple-element.58), kind=kLoop, calls=%fused_computation | loop fusion | flops 3145728 | bytes 2361344 | tf_op jit(solution)/shard_map/convert.4
  14.2 0.1 bitcast_dynamic-update-slice_fusion.1
  14.4 0.1 bitcast_dynamic-update-slice_fusion
  14.5 7.4 %collective-permute-done = bf16[2,64,12,64]{3,1,2,0:T(8,128)(2,1)S(1)} collective-permute-done((bf16[2,64,12,64]{3,1,2,0:T(8,128)(2,1)S(1)}, bf16[2,64,12,64]{3,1,2,0:T(8,128)(2,1)S(1)}, u32[]{:S(2)}, u32[]{:S(2)}) %collective-permute-start) | collective-permute-done | bytes 196640 | tf_op jit(solution)/shard_map/ppermute | solution.py:14
  22.0 0.1 copy.34
  22.1 0.2 reshape_squeeze.18
  22.5 0.2 reshape_squeeze.19
  22.6 0.4 fusion
  23.0 1.8 %collective-permute-start.1 = (bf16[2,64,12,64]{3,1,2,0:T(8,128)(2,1)S(1)}, bf16[2,64,12,64]{3,1,2,0:T(8,128)(2,1)}, u32[]{:S(2)}, u32[]{:S(2)}) collective-permute-start(bf16[2,64,12,64]{3,1,2,0:T(8,128)(2,1)S(1)} %collective-permute-done), channel_id=1, source_target_pairs={{0,12},{4,0},{8,4},{12,8},{1,13},{5,1},{9,5},{13,9},{2,14},{6,2},{... | collective-permute-start | bytes 589832 | tf_op jit(solution)/shard_map/ppermute | solution.py:14
  25.2 8.2 %collective-permute-done.1 = bf16[2,64,12,64]{3,1,2,0:T(8,128)(2,1)} collective-permute-done((bf16[2,64,12,64]{3,1,2,0:T(8,128)(2,1)S(1)}, bf16[2,64,12,64]{3,1,2,0:T(8,128)(2,1)}, u32[]{:S(2)}, u32[]{:S(2)}) %collective-permute-start.1) | collective-permute-done | bytes 196640 | tf_op jit(solution)/shard_map/ppermute | solution.py:14
  33.4 1.0 %fusion.22 = (bf16[1,64,12,64]{3,1,2,0:T(8,128)(2,1)S(1)}, bf16[1,64,12,64]{3,1,2,0:T(8,128)(2,1)S(1)}) fusion(bf16[2,64,12,64]{3,1,2,0:T(8,128)(2,1)} %collective-permute-done.1), kind=kLoop, calls=%fused_computation.49 | loop fusion | bytes 393216 | tf_op jit(solution)/shard_map/slice | solution.py:57
  34.5 0.1 copy.38
  34.6 0.2 reshape_squeeze.20
  34.8 0.1 copy.39
  35.0 0.2 reshape_squeeze.21
  35.1 0.4 fusion.4
  35.5 3.3 %collective-permute-start.2 = (bf16[2,64,12,64]{3,1,2,0:T(8,128)(2,1)}, bf16[2,64,12,64]{3,1,2,0:T(8,128)(2,1)}, u32[]{:S(2)}, u32[]{:S(2)}) collective-permute-start(bf16[2,64,12,64]{3,1,2,0:T(8,128)(2,1)} %collective-permute-done.1), channel_id=1, source_target_pairs={{0,12},{4,0},{8,4},{12,8},{1,13},{5,1},{9,5},{13,9},{2,14},{6,2},{... | collective-permute-start | bytes 589832 | tf_op jit(solution)/shard_map/ppermute | solution.py:14
  39.0 0.8 %copy.49 = f32[512,64]{1,0:T(8,128)} copy(f32[512,64]{0,1:T(8,128)S(1)} %get-tuple-element.49) | data formatting | bytes 262144 | tf_op jit(solution)/shard_map/stack | solution.py:63
  39.8 1.0 %pad_maximum_fusion = f32[2,4,128,64]{3,2,1,0:T(8,128)S(1)} fusion(f32[1,4,128,64]{3,2,1,0:T(8,128)} %bitcast.36, f32[1,4,128,64]{3,2,1,0:T(8,128)S(1)} %bitcast.33), kind=kLoop, calls=%fused_computation.7 | loop fusion | flops 65536 | bytes 524288 | tf_op jit(solution)/shard_map/stack | solution.py:63
  40.8 3.1 %scatter.11 = f32[2,4,128,192]{3,2,1,0:T(8,128)S(1)} dynamic-update-slice(f32[2,4,128,192]{3,2,1,0:T(8,128)S(1)} %select_maximum_fusion, f32[2,4,128,64]{3,2,1,0:T(8,128)S(1)} %pad_maximum_fusion, s32[]{:T(128)} %constant.120.clone.1, s32[]{:T(128)} %constant.120.clone.1, s32[]{:T(128)} %constant.120.clone.1, s32[]{:T(128)} %constant.118.clone.1) | dynamic-update-slice | bytes 524292 | tf_op jit(solution)/shard_map/scatter | solution.py:83
  43.9 1.9 %collective-permute-done.2 = bf16[2,64,12,64]{3,1,2,0:T(8,128)(2,1)} collective-permute-done((bf16[2,64,12,64]{3,1,2,0:T(8,128)(2,1)}, bf16[2,64,12,64]{3,1,2,0:T(8,128)(2,1)}, u32[]{:S(2)}, u32[]{:S(2)}) %collective-permute-start.2) | collective-permute-done | bytes 196640 | tf_op jit(solution)/shard_map/ppermute | solution.py:14
  45.8 1.0 %fusion.21 = (bf16[1,64,12,64]{3,1,2,0:T(8,128)(2,1)S(1)}, bf16[1,64,12,64]{3,1,2,0:T(8,128)(2,1)S(1)}) fusion(bf16[2,64,12,64]{3,1,2,0:T(8,128)(2,1)} %collective-permute-done.2), kind=kLoop, calls=%fused_computation.48 | loop fusion | bytes 393216 | tf_op jit(solution)/shard_map/slice | solution.py:57
  46.8 0.1 copy.42
  47.0 0.2 reshape_squeeze.22
  47.3 0.2 reshape_squeeze.23
  47.5 0.4 fusion.8
  48.2 1.0 %copy-done = f32[2,4,128,192]{3,2,1,0:T(8,128)} copy-done((f32[2,4,128,192]{3,2,1,0:T(8,128)}, f32[2,4,128,192]{3,2,1,0:T(8,128)S(1)}, u32[]{:S(2)}) %copy-start) | copy-done | bytes 786456
  49.2 26.8 %reduce-scatter.2.cloned.1.call-done = f32[2,4,32,192]{3,2,1,0:T(8,128)} async-done(((f32[2,4,128,192]{3,2,1,0:T(8,128)}), f32[2,4,32,192]{3,2,1,0:T(8,128)}) %reduce-scatter.2.cloned.1.call-update) | async-done | bytes 196624 | tf_op jit(solution)/shard_map/reduce_scatter | solution.py:90
  (21 shorter events, 1.6 us)
Async XLA Ops:
  6.5 69.5 %reduce-scatter.2.cloned.1.call-start = ((), (), s32[]{:S(2)}) async-start(), calls=%async_computation.1 | async-start | bytes 1310720 | tf_op jit(solution)/shard_map/reduce_scatter | solution.py:90
  7.7 14.2 %collective-permute-start = (bf16[2,64,12,64]{3,1,2,0:T(8,128)(2,1)S(1)}, bf16[2,64,12,64]{3,1,2,0:T(8,128)(2,1)S(1)}, u32[]{:S(2)}, u32[]{:S(2)}) collective-permute-start(bf16[2,64,12,64]{3,1,2,0:T(8,128)(2,1)S(1)} %bitcast.38), channel_id=1, source_target_pairs={{0,4},{4,8},{8,12},{12,0},{1,5},{5,9},{9,13},{13,1},{2,6},{6,10},{... | collective-permute-start | bytes 589832 | tf_op jit(solution)/shard_map/ppermute | solution.py:14
  23.0 10.4 %collective-permute-start.1 = (bf16[2,64,12,64]{3,1,2,0:T(8,128)(2,1)S(1)}, bf16[2,64,12,64]{3,1,2,0:T(8,128)(2,1)}, u32[]{:S(2)}, u32[]{:S(2)}) collective-permute-start(bf16[2,64,12,64]{3,1,2,0:T(8,128)(2,1)S(1)} %collective-permute-done), channel_id=1, source_target_pairs={{0,12},{4,0},{8,4},{12,8},{1,13},{5,1},{9,5},{13,9},{2,14},{6,2},{... | collective-permute-start | bytes 589832 | tf_op jit(solution)/shard_map/ppermute | solution.py:14
  35.5 10.3 %collective-permute-start.2 = (bf16[2,64,12,64]{3,1,2,0:T(8,128)(2,1)}, bf16[2,64,12,64]{3,1,2,0:T(8,128)(2,1)}, u32[]{:S(2)}, u32[]{:S(2)}) collective-permute-start(bf16[2,64,12,64]{3,1,2,0:T(8,128)(2,1)} %collective-permute-done.1), channel_id=1, source_target_pairs={{0,12},{4,0},{8,4},{12,8},{1,13},{5,1},{9,5},{13,9},{2,14},{6,2},{... | collective-permute-start | bytes 589832 | tf_op jit(solution)/shard_map/ppermute | solution.py:14
  48.2 1.0 %copy-start = (f32[2,4,128,192]{3,2,1,0:T(8,128)}, f32[2,4,128,192]{3,2,1,0:T(8,128)S(1)}, u32[]{:S(2)}) copy-start(f32[2,4,128,192]{3,2,1,0:T(8,128)S(1)} %maximum_dynamic-update-slice_fusion) | copy-start | bytes 2359300
Sparse Core Ops, SparseCore 0:
  49.3 26.6 reduce-scatter.1
where the time goes:
time: 83.2 us; the launch traced here: 82.9 us
  waiting for transfers between devices  44.4 us (53%)
  between operations  13.6 us (16%)
  local copies, waits for them, and re-layouts  10.9 us (13%)
  starting transfers between devices  8.21 us (10%)
  other arithmetic  4.6 us (6%)
  matrix products  1.13 us (1%)
    reduce_scatter x1, waiting for transfers between devices, shards(): return lax.psum_scatter(accum, 'site', scatter_dimension=2, tiled=True)  26.8 us
    ppermute x3, waiting for transfers between devices, shifted(): return lax.ppermute(value, axis, pairs)  17.6 us
    ppermute x3, starting transfers between devices, shifted(): return lax.ppermute(value, axis, pairs)  8.21 us
    scatter x1, local copies, waits for them, and re-layouts, handle(): return accum.at[:, :, :, column:column + vrows].set(part)  3.05 us
    slice x6, local copies, waits for them, and re-layouts, contract(): block[0].reshape(-1, width)  2.54 us
  transfers between devices with their start and end apart: 4, of which 4 were waited for; matrix products, arithmetic and copies ran while one was open for 11% of the time, Pallas kernels for 0%

commit v1 on v0

v1 whole, which is shorter than its diff:
```python
import jax
import jax.numpy as jnp
import numpy as np
from jax import lax
from jax.experimental import pallas as pl
from jax.experimental.pallas import tpu as pltpu
from jax.sharding import PartitionSpec as P

LAT = 96
REACH = 4
SPINS = 4
SIGNS = (-1.0, 1.0, 1.0, -1.0)


def shifted(value, axis, steps):
    count = lax.axis_size(axis)
    pairs = [(source, (source + steps) % count) for source in range(count)]
    return lax.ppermute(value, axis, pairs)


def peer(index, slot, count):
    if count & (count - 1) == 0:
        return index ^ slot
    return (index + slot) % count


def traded(value, axis, slot):
    count = lax.axis_size(axis)
    pairs = [(source, peer(source, slot, count)) for source in range(count)]
    return lax.ppermute(value, axis, pairs)


def make_phase(momenta, first, count):
    index = first + jnp.arange(count, dtype=jnp.int32)
    xcoord = index % LAT
    ycoord = index // LAT % LAT
    zcoord = index // (LAT * LAT)
    total = (
        momenta[:, 0:1] * xcoord[None, :]
        + momenta[:, 1:2] * ycoord[None, :]
        + momenta[:, 2:3] * zcoord[None, :]
    )
    wound = total % LAT
    angle = -2.0 * np.pi / LAT * wound.astype(jnp.float32)
    return (jnp.cos(angle), jnp.sin(angle))


def prepare_kernel(slots, nph, rows, owner_ref, w_ref, cos_ref, sin_ref, b_ref):
    wrows = w_ref.shape[3]
    sites = w_ref.shape[2]
    nsc = w_ref.shape[1]
    colours = nsc // SPINS
    wide = nph * rows
    lane = lax.broadcasted_iota(jnp.int32, (wrows, wide), 1) % rows
    line = lax.broadcasted_iota(jnp.int32, (wrows, wide), 0)
    picks = jnp.concatenate(
        [(line == lane + owner_ref[slot] * rows).astype(jnp.float32) for slot in range(slots)], axis=1
    ).astype(jnp.bfloat16)
    cosine = cos_ref[...]
    sine = sin_ref[...]
    for sc in range(nsc):
        spin, colour = divmod(sc, colours)
        other = (SPINS - 1 - spin) * colours + colour
        c, s = (cosine, sine) if SIGNS[SPINS - 1 - spin] > 0 else (-cosine, -sine)
        both = jnp.concatenate([w_ref[0, other], w_ref[1, other]], axis=0)
        spread = jnp.dot(both, picks, preferred_element_type=jnp.float32)
        for slot in range(slots):
            wreal = spread[:sites, slot * wide : (slot + 1) * wide]
            wimag = spread[sites:, slot * wide : (slot + 1) * wide]
            areal = wreal * c + wimag * s
            aimag = wreal * s - wimag * c
            low = areal.astype(jnp.bfloat16)
            high = aimag.astype(jnp.bfloat16)
            top = slice(sc * 2 * sites, (sc * 2 + 1) * sites)
            bottom = slice((sc * 2 + 1) * sites, (sc * 2 + 2) * sites)
            first = slice((2 * slot) * wide, (2 * slot + 1) * wide)
            second = slice((2 * slot + 1) * wide, (2 * slot + 2) * wide)
            b_ref[top, first] = low
            b_ref[bottom, first] = (-aimag).astype(jnp.bfloat16)
            b_ref[top, second] = high
            b_ref[bottom, second] = low


def contract_kernel(count, slots, *refs):
    blocks = refs[:count]
    b_ref = refs[count]
    outs = refs[count + 1 :]
    nsc = blocks[0].shape[0]
    vrows = blocks[0].shape[1]
    lhs = jnp.concatenate(
        [jnp.concatenate([block[sc] for sc in range(nsc)], axis=1) for block in blocks], axis=0
    )
    width = b_ref.shape[1] // slots
    for slot in range(slots):
        part = jnp.dot(lhs, b_ref[:, slot * width : (slot + 1) * width], preferred_element_type=jnp.float32)
        outs[slot][...] = part.astype(outs[slot].dtype)


def finish_kernel(order, groups, slots, vrows, *refs):
    out_ref = refs[-1]
    sums = []
    for group in range(groups):
        parts = refs[group * slots : (group + 1) * slots]
        total = parts[0][...]
        for part in parts[1:]:
            total = total + part[...].astype(jnp.float32)
        sums.append(total)
    band = [sums[group][row * vrows : (row + 1) * vrows] for group, row in order]
    out_ref[...] = jnp.concatenate(band, axis=0).T


VMEM = pl.BlockSpec(memory_space=pltpu.VMEM)
GRANT = 16 << 20


def local_call(body, name, out_shape, in_specs, flops, *operands):
    outs = out_shape if isinstance(out_shape, list) else [out_shape]
    moved = sum(int(np.prod(x.shape)) * x.dtype.itemsize for x in [*operands, *outs])
    return pl.pallas_call(
        body,
        out_shape=out_shape,
        in_specs=in_specs,
        out_specs=[VMEM] * len(outs) if isinstance(out_shape, list) else VMEM,
        name=name,
        cost_estimate=pl.CostEstimate(flops=flops, bytes_accessed=moved, transcendentals=0),
        compiler_params=pltpu.CompilerParams(vmem_limit_bytes=GRANT),
    )(*operands)


def shards(w_modes, v_modes, momenta):
    wrows = w_modes.shape[1]
    nsc = w_modes.shape[2]
    sites = w_modes.shape[3]
    vrows = v_modes.shape[1]
    nph = momenta.shape[0]
    nmode = lax.axis_size("mode")
    nsite = lax.axis_size("site")
    reach = min(REACH, (nmode - 1) // 2)
    rows = wrows // nsite
    width = 2 * nph * rows
    me = lax.axis_index("site")

    vt = jnp.transpose(v_modes, (0, 2, 1, 3))
    packed = jnp.concatenate([vt[0], vt[1]], axis=-1)
    offsets = [sign * step for step in range(1, reach + 1) for sign in (1, -1)]
    arrived = [shifted(packed, "mode", -offset) for offset in offsets]

    cosine, sine = make_phase(momenta, me * sites, sites)
    cosine = jnp.repeat(cosine.T, rows, axis=1)
    sine = jnp.repeat(sine.T, rows, axis=1)
    owners = jnp.stack([peer(me, slot, nsite) for slot in range(nsite)]).astype(jnp.int32)
    wt = jnp.transpose(w_modes, (0, 2, 3, 1))
    rhs = local_call(
        lambda *refs: prepare_kernel(nsite, nph, rows, *refs),
        "prepare",
        jax.ShapeDtypeStruct((nsc * 2 * sites, nsite * width), jnp.bfloat16),
        [pl.BlockSpec(memory_space=pltpu.SMEM), VMEM, VMEM, VMEM],
        2 * nsc * 2 * sites * wrows * nsite * nph * rows,
        owners,
        wt,
        cosine,
        sine,
    )

    def group_of(blocks):
        shape = (len(blocks) * vrows, width)
        parts = local_call(
            lambda *refs: contract_kernel(len(blocks), nsite, *refs),
            "contract",
            [jax.ShapeDtypeStruct(shape, jnp.float32)]
            + [jax.ShapeDtypeStruct(shape, jnp.bfloat16)] * (nsite - 1),
            [VMEM] * (len(blocks) + 1),
            2 * shape[0] * rhs.shape[0] * rhs.shape[1],
            *blocks,
            rhs,
        )
        return [parts[0]] + [traded(parts[slot], "site", slot) for slot in range(1, nsite)]

    first = group_of([packed])
    rest = group_of(arrived)
    place = {0: (0, 0)}
    for row, offset in enumerate(offsets):
        place[offset] = (1, row)
    order = [place[offset] for offset in range(-reach, reach + 1)]
    out = local_call(
        lambda *refs: finish_kernel(order, 2, nsite, vrows, *refs),
        "finish",
        jax.ShapeDtypeStruct((width, len(order) * vrows), jnp.float32),
        [VMEM] * (2 * nsite),
        0,
        *first,
        *rest,
    )
    return out.reshape(2, nph, rows, len(order) * vrows)


def solution(mesh):
    placed = (P(None, ("grp", "mode"), None, "site"), P(None, ("grp", "mode"), None, "site"), P())
    return jax.shard_map(
        shards,
        mesh=mesh,
        in_specs=placed,
        out_specs=P(None, None, ("grp", "mode", "site"), None),
        check_vma=False,
    )
```

time: 83.2 us -> 24.3 us (0.29)
  waiting for transfers between devices: 44.4 us -> 8.1 us
  between operations: 13.6 us -> 0.09 us
  local copies, waits for them, and re-layouts: 10.9 us -> 3.21 us
  other arithmetic: 4.6 us -> 0.39 us
  Pallas kernels: 0 us -> 3.53 us
  matrix products: 1.13 us -> 0 us
    reduce_scatter x1 -> x0, waiting for transfers between devices: 26.8 us -> none  [shards(): return lax.psum_scatter(accum, 'site', scatter_dimension=2, tiled=True)]
    ppermute x3 -> x2, waiting for transfers between devices: 17.6 us -> 4.63 us  [shifted(): return lax.ppermute(value, axis, pairs)]
    ppermute x0 -> x6, starting transfers between devices: none -> 3.7 us  [traded(): return lax.ppermute(value, axis, pairs)]
    pallas_call x0 -> x4, Pallas kernels: none -> 3.53 us  [local_call(): pl.pallas_call(body, out_shape=out_shape, in_specs=in_specs, out_specs=[V...]
    ppermute x0 -> x6, waiting for transfers between devices: none -> 3.47 us  [traded(): return lax.ppermute(value, axis, pairs)]
    ppermute x3 -> x2, starting transfers between devices: 8.21 us -> 5.13 us  [shifted(): return lax.ppermute(value, axis, pairs)]
    scatter x1 -> x0, local copies, waits for them, and re-layouts: 3.05 us -> none  [handle(): return accum.at[:, :, :, column:column + vrows].set(part)]
    slice x9 -> x0, local copies, waits for them, and re-layouts: 2.95 us -> none  [the longest x6 2.54 us: contract(): block[0].reshape(-1, width)]
  transfers between devices with their start and end apart: 4 -> 8, of which waited for: 4 -> 4; matrix products, arithmetic and copies ran while one was open for 11% -> 6% of each run, Pallas kernels for 0% -> 11%
where the time goes in v1:
time: 24.3 us; the launch traced here: 24.1 us
  starting transfers between devices  8.83 us (36%)
  waiting for transfers between devices  8.1 us (33%)
  Pallas kernels  3.53 us (15%)
  local copies, waits for them, and re-layouts  3.21 us (13%)
  other arithmetic  0.39 us (2%)
    ppermute x2, starting transfers between devices, shifted(): return lax.ppermute(value, axis, pairs)  5.13 us
    ppermute x2, waiting for transfers between devices, shifted(): return lax.ppermute(value, axis, pairs)  4.63 us
    ppermute x6, starting transfers between devices, traded(): return lax.ppermute(value, axis, pairs)  3.7 us
    pallas_call x4, Pallas kernels, local_call(): pl.pallas_call(body, out_shape=out_shape, in_specs=in_specs, out_specs=[V...  3.53 us
    ppermute x6, waiting for transfers between devices, traded(): return lax.ppermute(value, axis, pairs)  3.47 us
    squeeze x1, local copies, waits for them, and re-layouts, shards(): packed = jnp.concatenate([vt[0], vt[1]], axis=-1)  1.05 us
    slice x1, local copies, waits for them, and re-layouts, make_phase(): momenta[:, 0:1] * xcoord[None, :] + momenta[:, 1:2] * ycoord[None, :]  1.01 us
    unnamed x2, local copies, waits for them, and re-layouts  1 us
  transfers between devices with their start and end apart: 8, of which 4 were waited for; matrix products, arithmetic and copies ran while one was open for 6% of the time, Pallas kernels for 11%

profile of v1, /device:TPU:0, one launch (start us, length us, event | category | flops | bytes accessed | tf_op | source)
XLA Modules:
  0.0 24.1 jit_solution(5292702077649640185)
XLA Ops:
  0.0 1.0 %slice_bitcast_fusion.1 = (bf16[12,64,64]{2,1,0:T(8,128)(2,1)S(1)}, bf16[12,64,64]{2,1,0:T(8,128)(2,1)S(1)}) fusion(bf16[2,12,64,64]{3,2,1,0:T(8,128)(2,1)} %bitcast.14), kind=kLoop, calls=%fused_computation.1 | loop fusion | bytes 393216 | tf_op jit(solution)/shard_map/squeeze | solution.py:144
  1.1 0.1 pad_maximum_fusion.refs_0_
  1.2 5.1 %collective-permute-start.3 = (bf16[12,64,128]{2,1,0:T(8,128)(2,1)S(1)}, bf16[12,64,128]{2,1,0:T(8,128)(2,1)S(1)}, u32[]{:S(2)}, u32[]{:S(2)}) collective-permute-start(bf16[12,64,128]{2,1,0:T(8,128)(2,1)S(1)} %pad_maximum_fusion.refs_0_), channel_id=1, source_target_pairs={{0,12},{4,0},{8,4},{12,8},{1,13},{5,1},{9,5},{13,9},{2,14},{6,2},{... | collective-permute-start | bytes 589832 | tf_op jit(solution)/shard_map/ppermute | solution.py:18
  6.3 0.0 collective-permute-start.4
  6.4 1.0 %slice_reduce_fusion.2 = (s32[4]{0:T(128)S(1)}, s32[4]{0:T(128)S(1)}, s32[4]{0:T(128)S(1)}) fusion(s32[4,3]{1,0:T(4,128)} %param.5), kind=kLoop, calls=%fused_computation.9 | loop fusion | bytes 96 | tf_op jit(solution)/shard_map/slice | solution.py:39
  7.4 0.1 fusion.4
  7.5 0.1 copy.4.refs_2_
  7.6 0.1 copy.5.refs_3_
  7.7 0.1 pad_add_fusion.refs_0_
  7.8 0.0 copy-start
  7.8 1.0 %copy-done = bf16[2,128,12,64]{1,3,2,0:T(8,128)(2,1)S(1)} copy-done((bf16[2,128,12,64]{1,3,2,0:T(8,128)(2,1)S(1)}, bf16[2,128,12,64]{1,3,2,0:T(8,128)(2,1)}, u32[]{:S(2)}) %copy-start) | copy-done | bytes 393240
  8.8 1.4 %prepare.1.refs_1_.refs_2_ = bf16[1536,1024]{1,0:T(8,128)(2,1)S(1)} custom-call(s32[4]{0:T(128)S(1)} %pad_add_fusion.refs_0_, bf16[2,12,64,128]{3,2,1,0:T(8,128)(2,1)S(1)} %bitcast.13, f32[64,128]{1,0:T(8,128)S(1)} %copy.4.refs_2_, f32[64,128]{1,0:T(8,128)S(1)} %copy.5.refs_3_), custom_call_target="tpu_custom_call" | custom-call | flops 201326592 | bytes 3604496 | tf_op jit(solution)/shard_map/prepare/pallas_call | solution.py:119
  10.2 0.7 %contract.2 = (f32[64,256]{1,0:T(8,128)S(1)}, bf16[64,256]{1,0:T(8,128)(2,1)S(1)}, bf16[64,256]{1,0:T(8,128)(2,1)S(1)}, bf16[64,256]{1,0:T(8,128)(2,1)S(1)}) custom-call(bf16[12,64,128]{2,1,0:T(8,128)(2,1)S(1)} %pad_maximum_fusion.refs_0_, bf16[1536,1024]{1,0:T(8,128)(2,1)S(1)} %prepare.1.refs_1_.refs_2_), custom_call_target="tpu_custom_call" | custom-call | flops 201326592 | bytes 3506176 | tf_op jit(solution)/shard_map/contract/pallas_call | solution.py:119
  10.9 0.1 collective-permute-start
  11.0 0.6 %collective-permute-done.3.refs_0_ = bf16[12,64,128]{2,1,0:T(8,128)(2,1)S(1)} collective-permute-done((bf16[12,64,128]{2,1,0:T(8,128)(2,1)S(1)}, bf16[12,64,128]{2,1,0:T(8,128)(2,1)S(1)}, u32[]{:S(2)}, u32[]{:S(2)}) %collective-permute-start.3) | collective-permute-done | bytes 196640 | tf_op jit(solution)/shard_map/ppermute | solution.py:18
  11.6 4.0 %collective-permute-done.4.refs_1_ = bf16[12,64,128]{2,1,0:T(8,128)(2,1)S(1)} collective-permute-done((bf16[12,64,128]{2,1,0:T(8,128)(2,1)S(1)}, bf16[12,64,128]{2,1,0:T(8,128)(2,1)S(1)}, u32[]{:S(2)}, u32[]{:S(2)}) %collective-permute-start.4) | collective-permute-done | bytes 196640 | tf_op jit(solution)/shard_map/ppermute | solution.py:18
  15.6 0.6 %contract.3 = (f32[128,256]{1,0:T(8,128)S(1)}, bf16[128,256]{1,0:T(8,128)(2,1)S(1)}, bf16[128,256]{1,0:T(8,128)(2,1)S(1)}, bf16[128,256]{1,0:T(8,128)(2,1)S(1)}) custom-call(bf16[12,64,128]{2,1,0:T(8,128)(2,1)S(1)} %collective-permute-done.3.refs_0_, bf16[12,64,128]{2,1,0:T(8,128)(2,1)S(1)} %collective-permute-done.4.refs_1_, ...), custom_call_target="tpu_custom_call" | custom-call | flops 402653184 | bytes 3866624 | tf_op jit(solution)/shard_map/contract/pallas_call | solution.py:119
  16.2 0.1 collective-permute-start.5
  16.3 1.6 %collective-permute-start.6 = (bf16[128,256]{1,0:T(8,128)(2,1)S(1)}, bf16[128,256]{1,0:T(8,128)(2,1)S(1)}, u32[]{:S(2)}, u32[]{:S(2)}) collective-permute-start(bf16[128,256]{1,0:T(8,128)(2,1)S(1)} %get-tuple-element.19), channel_id=1, source_target_pairs={{0,2},{1,3},{2,0},{3,1},{4,6},{5,7},{6,4},{7,5},{8,10},{9,11},{10,... | collective-permute-start | bytes 196616 | tf_op jit(solution)/shard_map/ppermute | solution.py:30
  17.8 0.3 %collective-permute-start.7 = (bf16[128,256]{1,0:T(8,128)(2,1)S(1)}, bf16[128,256]{1,0:T(8,128)(2,1)S(1)}, u32[]{:S(2)}, u32[]{:S(2)}) collective-permute-start(bf16[128,256]{1,0:T(8,128)(2,1)S(1)} %get-tuple-element.20), channel_id=1, source_target_pairs={{0,3},{1,2},{2,1},{3,0},{4,7},{5,6},{6,5},{7,4},{8,11},{9,10},{10,... | collective-permute-start | bytes 196616 | tf_op jit(solution)/shard_map/ppermute | solution.py:30
  18.1 1.5 %collective-permute-start.1 = (bf16[64,256]{1,0:T(8,128)(2,1)S(1)}, bf16[64,256]{1,0:T(8,128)(2,1)S(1)}, u32[]{:S(2)}, u32[]{:S(2)}) collective-permute-start(bf16[64,256]{1,0:T(8,128)(2,1)S(1)} %get-tuple-element.15), channel_id=1, source_target_pairs={{0,2},{1,3},{2,0},{3,1},{4,6},{5,7},{6,4},{7,5},{8,10},{9,11},{10,... | collective-permute-start | bytes 98312 | tf_op jit(solution)/shard_map/ppermute | solution.py:30
  19.6 0.0 collective-permute-done.refs_1_
  19.6 0.2 collective-permute-start.2
  19.8 3.4 %collective-permute-done.1.refs_2_ = bf16[64,256]{1,0:T(8,128)(2,1)S(1)} collective-permute-done((bf16[64,256]{1,0:T(8,128)(2,1)S(1)}, bf16[64,256]{1,0:T(8,128)(2,1)S(1)}, u32[]{:S(2)}, u32[]{:S(2)}) %collective-permute-start.1) | collective-permute-done | bytes 32800 | tf_op jit(solution)/shard_map/ppermute | solution.py:30
  23.2 0.1 collective-permute-done.2.refs_3_
  23.3 0.0 collective-permute-done.5.refs_5_
  23.3 0.0 collective-permute-done.6.refs_6_
  23.3 0.0 collective-permute-done.7.refs_7_
  23.3 0.8 %finish.1 = f32[256,192]{1,0:T(8,128)} custom-call(f32[64,256]{1,0:T(8,128)S(1)} %get-tuple-element.13.refs_0_, bf16[64,256]{1,0:T(8,128)(2,1)S(1)} %collective-permute-done.refs_1_, bf16[64,256]{1,0:T(8,128)(2,1)S(1)} %collective-permute-done.1.refs_2_, bf16[64,256]{1,0:T(8,128)(2,1)S(1)} %collective-permute-done.2.refs_3_, ...), custom_call_target="tpu_custom_call" | custom-call | bytes 688128 | tf_op jit(solution)/shard_map/finish/pallas_call | solution.py:119
  (4 shorter events, 0.1 us)
Async XLA Ops:
  1.2 10.4 %collective-permute-start.3 = (bf16[12,64,128]{2,1,0:T(8,128)(2,1)S(1)}, bf16[12,64,128]{2,1,0:T(8,128)(2,1)S(1)}, u32[]{:S(2)}, u32[]{:S(2)}) collective-permute-start(bf16[12,64,128]{2,1,0:T(8,128)(2,1)S(1)} %pad_maximum_fusion.refs_0_), channel_id=1, source_target_pairs={{0,12},{4,0},{8,4},{12,8},{1,13},{5,1},{9,5},{13,9},{2,14},{6,2},{... | collective-permute-start | bytes 589832 | tf_op jit(solution)/shard_map/ppermute | solution.py:18
  6.3 9.3 %collective-permute-start.4 = (bf16[12,64,128]{2,1,0:T(8,128)(2,1)S(1)}, bf16[12,64,128]{2,1,0:T(8,128)(2,1)S(1)}, u32[]{:S(2)}, u32[]{:S(2)}) collective-permute-start(bf16[12,64,128]{2,1,0:T(8,128)(2,1)S(1)} %pad_maximum_fusion.refs_0_), channel_id=1, source_target_pairs={{0,4},{4,8},{8,12},{12,0},{1,5},{5,9},{9,13},{13,1},{2,6},{6,10},{... | collective-permute-start | bytes 589832 | tf_op jit(solution)/shard_map/ppermute | solution.py:18
  7.8 1.0 %copy-start = (bf16[2,128,12,64]{1,3,2,0:T(8,128)(2,1)S(1)}, bf16[2,128,12,64]{1,3,2,0:T(8,128)(2,1)}, u32[]{:S(2)}) copy-start(bf16[2,128,12,64]{1,3,2,0:T(8,128)(2,1)} %param.3) | copy-start | bytes 1179652
  10.9 8.7 %collective-permute-start = (bf16[64,256]{1,0:T(8,128)(2,1)S(1)}, bf16[64,256]{1,0:T(8,128)(2,1)S(1)}, u32[]{:S(2)}, u32[]{:S(2)}) collective-permute-start(bf16[64,256]{1,0:T(8,128)(2,1)S(1)} %get-tuple-element.14), channel_id=1, source_target_pairs={{0,1},{1,0},{2,3},{3,2},{4,5},{5,4},{6,7},{7,6},{8,9},{9,8},{10,11... | collective-permute-start | bytes 98312 | tf_op jit(solution)/shard_map/ppermute | solution.py:30
  16.2 7.1 %collective-permute-start.5 = (bf16[128,256]{1,0:T(8,128)(2,1)S(1)}, bf16[128,256]{1,0:T(8,128)(2,1)S(1)}, u32[]{:S(2)}, u32[]{:S(2)}) collective-permute-start(bf16[128,256]{1,0:T(8,128)(2,1)S(1)} %get-tuple-element.18), channel_id=1, source_target_pairs={{0,1},{1,0},{2,3},{3,2},{4,5},{5,4},{6,7},{7,6},{8,9},{9,8},{10,11... | collective-permute-start | bytes 196616 | tf_op jit(solution)/shard_map/ppermute | solution.py:30
  16.3 7.0 %collective-permute-start.6 = (bf16[128,256]{1,0:T(8,128)(2,1)S(1)}, bf16[128,256]{1,0:T(8,128)(2,1)S(1)}, u32[]{:S(2)}, u32[]{:S(2)}) collective-permute-start(bf16[128,256]{1,0:T(8,128)(2,1)S(1)} %get-tuple-element.19), channel_id=1, source_target_pairs={{0,2},{1,3},{2,0},{3,1},{4,6},{5,7},{6,4},{7,5},{8,10},{9,11},{10,... | collective-permute-start | bytes 196616 | tf_op jit(solution)/shard_map/ppermute | solution.py:30
  17.8 5.5 %collective-permute-start.7 = (bf16[128,256]{1,0:T(8,128)(2,1)S(1)}, bf16[128,256]{1,0:T(8,128)(2,1)S(1)}, u32[]{:S(2)}, u32[]{:S(2)}) collective-permute-start(bf16[128,256]{1,0:T(8,128)(2,1)S(1)} %get-tuple-element.20), channel_id=1, source_target_pairs={{0,3},{1,2},{2,1},{3,0},{4,7},{5,6},{6,5},{7,4},{8,11},{9,10},{10,... | collective-permute-start | bytes 196616 | tf_op jit(solution)/shard_map/ppermute | solution.py:30
  18.1 5.1 %collective-permute-start.1 = (bf16[64,256]{1,0:T(8,128)(2,1)S(1)}, bf16[64,256]{1,0:T(8,128)(2,1)S(1)}, u32[]{:S(2)}, u32[]{:S(2)}) collective-permute-start(bf16[64,256]{1,0:T(8,128)(2,1)S(1)} %get-tuple-element.15), channel_id=1, source_target_pairs={{0,2},{1,3},{2,0},{3,1},{4,6},{5,7},{6,4},{7,5},{8,10},{9,11},{10,... | collective-permute-start | bytes 98312 | tf_op jit(solution)/shard_map/ppermute | solution.py:30
  19.6 3.7 %collective-permute-start.2 = (bf16[64,256]{1,0:T(8,128)(2,1)S(1)}, bf16[64,256]{1,0:T(8,128)(2,1)S(1)}, u32[]{:S(2)}, u32[]{:S(2)}) collective-permute-start(bf16[64,256]{1,0:T(8,128)(2,1)S(1)} %get-tuple-element.16), channel_id=1, source_target_pairs={{0,3},{1,2},{2,1},{3,0},{4,7},{5,6},{6,5},{7,4},{8,11},{9,10},{10,... | collective-permute-start | bytes 98312 | tf_op jit(solution)/shard_map/ppermute | solution.py:30
